TPU v7x, 256 devices: a whole 4x4x8 slice. The times are simulated.
256 devices in a mesh: enc: 16 (over z, core), vocab: 8 (over x, y_hi), grp: 2 (over y_lo).
Axes of the slice: x: 4, y: 4 (y_hi: 2, y_lo: 2; y = y_hi * 2 + y_lo), z: 8, core: 2. Of those that a mesh axis runs over, the one named last changes fastest.
Arguments:
- hidden: bfloat16 [12288, 1024], P('enc', ('vocab', 'grp')), may hold values from -6 to 6
- dense_weight: bfloat16 [1024, 1024], P('enc'), may hold values from -0.1875 to 0.1875
- head_weight: bfloat16 [1024, 126976], P('enc', ('vocab', 'grp')), may hold values from -0.1875 to 0.1875
- head_bias: float32 [126976], P(('vocab', 'grp')), may hold values from -4 to 4
- lengths: int32 [48], P('enc'), may hold values from 64 to 256, as said below
- queries: bfloat16 [128, 126976], P('enc', ('vocab', 'grp')), may hold values from -0.25 to 0.25283518
- positives: int32 [128], replicated, may hold values from 0 to 47
Outputs:
- batch_loss: float32 [], replicated
- query_grad: float32 [128, 126976], P('enc', ('vocab', 'grp'))
- passage_grad: float32 [48, 126976], P('enc', ('vocab', 'grp'))
Inputs may be any that keep to these rules, and one draw needn't show every extreme that they name: `lengths`: each 3 passages in a row hold, among their first two, one with 256 valid tokens and one with 64.
All inputs are finite; a program needn't handle non-finite values.
Results may differ from a plain program's by a relative error of at most 0.035.
Values may be sent and summed in bfloat16 or wider, within the bound.
A program may use at most 128 MiB of HBM per device.

v0:
```python
import jax
import jax.numpy as jnp
from jax import lax
from jax.sharding import PartitionSpec as P


def finish_norm(pre_act):
    activated = jax.nn.gelu(pre_act, approximate=False)
    center = jnp.mean(activated, axis=-1, keepdims=True)
    spread = jnp.mean(jnp.square(activated - center), axis=-1, keepdims=True)
    return ((activated - center) * lax.rsqrt(spread + 1e-05)).astype(jnp.bfloat16)


def project(in_rows, dense_weight):
    pre_act = jnp.dot(
        in_rows,
        lax.all_gather(dense_weight, "enc", axis=0, tiled=True),
        preferred_element_type=jnp.float32,
    )
    return finish_norm(pre_act)


def pool_reps(logits, token_counts, seq_len):
    passages = token_counts.shape[0]
    by_passage = logits.reshape(passages, seq_len, logits.shape[1])
    positions = lax.broadcasted_iota(jnp.int32, (passages, seq_len), 1)
    is_valid = positions < token_counts[:, None]
    masked = jnp.where(is_valid[:, :, None], by_passage, -jnp.inf)
    peak_val = jnp.max(masked, axis=1)
    return jnp.log1p(jnp.maximum(peak_val, 0.0)).astype(jnp.bfloat16)


def softmax_grads(scores, chosen):
    peak_val = jnp.max(scores, axis=1, keepdims=True)
    log_total = jnp.log(jnp.sum(jnp.exp(scores - peak_val), axis=1, keepdims=True)) + peak_val
    columns = lax.broadcasted_iota(jnp.int32, scores.shape, 1)
    is_positive = columns == chosen[:, None]
    picked_score = jnp.sum(jnp.where(is_positive, scores, 0.0), axis=1)
    batch_loss = jnp.sum(log_total[:, 0] - picked_score)
    score_grad = (jnp.exp(scores - log_total) - is_positive.astype(jnp.float32)).astype(
        jnp.bfloat16
    )
    return (batch_loss, score_grad)


def per_device(hidden, dense_weight, head_weight, head_bias, lengths, queries, positives):
    pass_dev = lengths.shape[0]
    seq_len = hidden.shape[0] // pass_dev
    enc_index = lax.axis_index("enc")
    features_all = lax.all_gather(hidden, ("vocab", "grp"), axis=1, tiled=True)
    normed = project(features_all, dense_weight)
    logits = jnp.dot(
        normed,
        lax.all_gather(head_weight, "enc", axis=0, tiled=True),
        preferred_element_type=jnp.float32,
    )
    pass_reps = pool_reps(logits + head_bias, lengths, seq_len)
    all_queries = lax.all_gather(queries, "enc", axis=0, tiled=True)
    partial_value = lax.dot_general(
        all_queries, pass_reps, (((1,), (1,)), ((), ())), preferred_element_type=jnp.float32
    )
    local_scores = lax.psum(partial_value, ("vocab", "grp"))
    scores = lax.all_gather(local_scores, "enc", axis=1, tiled=True)
    loss_sum, score_grad = softmax_grads(scores, positives)
    batch_loss = loss_sum / scores.shape[0]
    own_grad = lax.dynamic_slice_in_dim(score_grad, enc_index * pass_dev, pass_dev, 1)
    query_grad = lax.psum_scatter(
        jnp.dot(own_grad, pass_reps, preferred_element_type=jnp.float32),
        "enc",
        scatter_dimension=0,
        tiled=True,
    )
    passage_grad = lax.dot_general(
        own_grad, all_queries, (((0,), (0,)), ((), ())), preferred_element_type=jnp.float32
    )
    return (batch_loss, query_grad, passage_grad)


def solution(mesh):
    placed = (
        P("enc", ("vocab", "grp")),
        P("enc", None),
        P("enc", ("vocab", "grp")),
        P(("vocab", "grp")),
        P("enc"),
        P("enc", ("vocab", "grp")),
        P(),
    )
    return jax.shard_map(
        per_device,
        mesh=mesh,
        in_specs=placed,
        out_specs=(P(), P("enc", ("vocab", "grp")), P("enc", ("vocab", "grp"))),
        check_vma=False,
    )
```

profile of v0, /device:TPU:2, one launch (start us, length us, event | category | flops | bytes accessed | tf_op | source)
XLA Modules:
  0.0 363.2 jit_solution(3995243074012879067)
XLA Ops:
  7.2 0.0 all-gather.6.cloned.1.call-start
  7.2 0.7 all-gather.6.cloned.1.call-update
  7.9 0.0 all-gather.8.cloned.1.call-start
  7.9 0.7 all-gather.8.cloned.1.call-update
  8.6 0.0 all-gather.10.cloned.1.call-start
  8.7 0.7 all-gather.10.cloned.1.call-update
  9.4 0.0 all-gather.12.cloned.1.call-start
  9.4 0.5 all-gather.12.cloned.1.call-update
  10.0 0.0 reduce-scatter.2.cloned.1.call-start
  10.0 0.7 iota_compare_fusion.1
  10.7 0.7 iota_compare_fusion
  11.4 50.6 %all-gather.6.cloned.1.call-done = bf16[768,1024]{0,1:T(8,128)(2,1)} async-done(((bf16[768,64]{0,1:T(8,128)(2,1)}), bf16[768,1024]{0,1:T(8,128)(2,1)}) %all-gather.6.cloned.1.call-update) | async-done | bytes 1572880 | tf_op jit(solution)/shard_map/all_gather | solution.py:50
  62.0 41.4 %all-gather.8.cloned.1.call-done = bf16[1024,1024]{1,0:T(8,128)(2,1)} async-done(((bf16[64,1024]{1,0:T(8,128)(2,1)}), bf16[1024,1024]{1,0:T(8,128)(2,1)}) %all-gather.8.cloned.1.call-update) | async-done | bytes 2097168 | tf_op jit(solution)/shard_map/all_gather | solution.py:17
  103.4 10.5 %fusion.17 = (f32[768]{0:T(1024)S(1)}, f32[768,1024]{1,0:T(8,128)S(1)}) fusion(bf16[768,1024]{0,1:T(8,128)(2,1)} %all-gather.6.cloned.1.call-done, bf16[1024,1024]{1,0:T(8,128)(2,1)} %all-gather.8.cloned.1.call-done), kind=kOutput, calls=%fused_computation.41 | convolution fusion | flops 1661730048 | bytes 6818816 | tf_op jit(solution)/shard_map/dot_general | solution.py:15
  114.0 0.0 copy-start.2
  114.0 0.4 multiply_reduce_fusion
  114.5 82.1 %all-gather.10.cloned.1.call-done = bf16[1024,7936]{1,0:T(8,128)(2,1)} async-done(((bf16[64,7936]{1,0:T(8,128)(2,1)}), bf16[1024,7936]{1,0:T(8,128)(2,1)}) %all-gather.10.cloned.1.call-update) | async-done | bytes 16252944 | tf_op jit(solution)/shard_map/all_gather | solution.py:54
  196.5 0.0 copy-done.2
  196.5 21.4 %convolution_add_fusion = f32[768,7936]{1,0:T(8,128)} fusion(bf16[1024,7936]{1,0:T(8,128)(2,1)} %all-gather.10.cloned.1.call-done, f32[7936]{0:T(1024)S(1)} %copy-done.2, f32[768,1024]{1,0:T(8,128)S(1)} %get-tuple-element.8, f32[768]{0:T(1024)S(1)} %add_rsqrt_fusion, f32[768]{0:T(1024)S(1)} %broadcast_multiply_fusion), kind=kOutput, calls=%fused_computation.1 | convolution fusion | flops 12490702848 | bytes 43815936 | tf_op jit(solution)/shard_map/dot_general | solution.py:52
  217.9 0.0 copy-start.1
  217.9 9.4 %select_reduce_fusion = f32[3,7936]{1,0:T(4,128)S(1)} fusion(f32[3,256,7936]{2,1,0:T(8,128)} %bitcast.14, pred[3,256]{1,0:T(4,128)(4,1)S(1)} %iota_compare_fusion.1), kind=kLoop, calls=%fused_computation | loop fusion | flops 12165888 | bytes 24475392 | tf_op jit(solution)/shard_map/reduce_max | solution.py:29
  227.4 9.2 %all-gather.12.cloned.1.call-done = bf16[128,7936]{1,0:T(8,128)(2,1)} async-done(((bf16[8,7936]{1,0:T(8,128)(2,1)}), bf16[128,7936]{1,0:T(8,128)(2,1)}) %all-gather.12.cloned.1.call-update) | async-done | bytes 2031632 | tf_op jit(solution)/shard_map/all_gather | solution.py:58
  236.5 2.2 convolution_bitcast_fusion
  238.7 34.3 %psum.7 = f32[128,3]{0,1:T(4,128)S(1)} all-reduce(f32[128,3]{0,1:T(4,128)S(1)} %convolution_bitcast_fusion), channel_id=1, replica_groups=mesh['enc'=16,'vocab'=8,'grp'=2] {'vocab','grp'}, use_global_device_ids=true, to_apply=%region_3.4 | all-reduce | flops 384 | bytes 3072 | tf_op jit(solution)/shard_map/psum | solution.py:62
  273.0 15.7 %all-gather = f32[16,3,128]{2,1,0:T(4,128)S(1)} all-gather(f32[1,3,128]{2,1,0:T(4,128)S(1)} %bitcast.17), channel_id=1, replica_groups=mesh['enc'=16,'vocab'=8,'grp'=2] {'enc'}, dimensions={0}, use_global_device_ids=true | all-gather | bytes 26112 | tf_op jit(solution)/shard_map/all_gather | solution.py:63
  288.7 0.0 copy-done.1
  288.8 0.6 subtract_reduce_fusion
  289.4 2.7 fusion.14
  292.0 0.0 reduce-scatter.2.cloned.1.call-update
  292.7 0.0 copy-done
  292.7 1.0 fusion.20
  293.8 61.7 %reduce-scatter.2.cloned.1.call-done = f32[8,7936]{1,0:T(8,128)} async-done(((f32[128,7936]{1,0:T(8,128)}), f32[8,7936]{1,0:T(8,128)}) %reduce-scatter.2.cloned.1.call-update) | async-done | bytes 253968 | tf_op jit(solution)/shard_map/reduce_scatter | solution.py:67
  (6 shorter events, 0.1 us)
Async XLA Ops:
  7.2 54.9 %all-gather.6.cloned.1.call-start = ((), (), s32[]{:S(2)}) async-start(), calls=%async_computation.1 | async-start | bytes 1671168 | tf_op jit(solution)/shard_map/all_gather | solution.py:50
  7.9 95.5 %all-gather.8.cloned.1.call-start = ((), (), s32[]{:S(2)}) async-start(), calls=%async_computation.2 | async-start | bytes 2228224 | tf_op jit(solution)/shard_map/all_gather | solution.py:17
  8.6 187.9 %all-gather.10.cloned.1.call-start = ((), (), s32[]{:S(2)}) async-start(), calls=%async_computation.3 | async-start | bytes 17268736 | tf_op jit(solution)/shard_map/all_gather | solution.py:54
  9.4 227.2 %all-gather.12.cloned.1.call-start = ((), (), s32[]{:S(2)}) async-start(), calls=%async_computation.4 | async-start | bytes 2158592 | tf_op jit(solution)/shard_map/all_gather | solution.py:58
  10.0 345.5 %reduce-scatter.2.cloned.1.call-start = ((), (), s32[]{:S(2)}) async-start(), calls=%async_computation.5 | async-start | bytes 4317184 | tf_op jit(solution)/shard_map/reduce_scatter | solution.py:67
  114.0 82.6 %copy-start.2 = (f32[7936]{0:T(1024)S(1)}, f32[7936]{0:T(1024)}, u32[]{:S(2)}) copy-start(f32[7936]{0:T(1024)} %param.10) | copy-start | bytes 95236
  217.9 70.8 %copy-start.1 = (s32[128]{0:T(128)S(1)}, s32[128]{0:T(128)}, u32[]{:S(2)}) copy-start(s32[128]{0:T(128)} %param.13) | copy-start | bytes 1540
  289.4 3.3 copy-start
Sparse Core Ops, SparseCore 0:
  10.5 51.5 all-gather.5
  63.9 39.5 all-gather.7
  105.3 91.2 all-gather.9
  198.2 38.2 all-gather.11
  292.2 63.2 reduce-scatter.1
where the time goes:
time: 363 us
  waiting for transfers between devices  248 us (68%)
  blocking collectives  50 us (14%)
  matrix products  37.8 us (10%)
  between operations  15.6 us (4%)
  other arithmetic  12 us (3%)
    all_gather x1, waiting for transfers between devices, per_device(): lax.all_gather(head_weight, 'enc', axis=0, tiled=True)  82.1 us
    reduce_scatter x1, waiting for transfers between devices, per_device(): lax.psum_scatter(jnp.dot(own_grad, pass_reps, preferred_element_type=jnp....  61.7 us
    all_gather x1, waiting for transfers between devices, per_device(): features_all = lax.all_gather(hidden, ('vocab', 'grp'), axis=1, tiled=True)  50.6 us
    all_gather x1, waiting for transfers between devices, project(): lax.all_gather(dense_weight, 'enc', axis=0, tiled=True)  41.4 us
    psum x1, blocking collectives, per_device(): local_scores = lax.psum(partial_value, ('vocab', 'grp'))  34.3 us
    dot_general x1, matrix products, per_device(): jnp.dot(normed, lax.all_gather(head_weight, 'enc', axis=0, tiled=True), p...  21.4 us
    all_gather x1, blocking collectives, per_device(): scores = lax.all_gather(local_scores, 'enc', axis=1, tiled=True)  15.7 us
    dot_general x1, matrix products, project(): jnp.dot(in_rows, lax.all_gather(dense_weight, 'enc', axis=0, tiled=True),...  10.5 us
  transfers between devices with their start and end apart: 5, of which 5 were waited for; matrix products, arithmetic and copies ran while one was open for 12% of the time, Pallas kernels for 0%

commit v1 on v0

--- a/solution.py
+++ b/solution.py
@@ -2,6 +2,14 @@
 import jax.numpy as jnp
 from jax import lax
 from jax.sharding import PartitionSpec as P
+
+
+def gather_from_all(shard, axis, dim):
+    devices = lax.axis_size(axis)
+    repeats = [devices if d == dim else 1 for d in range(shard.ndim)]
+    return lax.all_to_all(
+        jnp.tile(shard, repeats), axis, split_axis=dim, concat_axis=dim, tiled=True
+    )
 
 
 def finish_norm(pre_act):
@@ -50,9 +58,7 @@
     features_all = lax.all_gather(hidden, ("vocab", "grp"), axis=1, tiled=True)
     normed = project(features_all, dense_weight)
     logits = jnp.dot(
-        normed,
-        lax.all_gather(head_weight, "enc", axis=0, tiled=True),
-        preferred_element_type=jnp.float32,
+        normed, gather_from_all(head_weight, "enc", 0), preferred_element_type=jnp.float32
     )
     pass_reps = pool_reps(logits + head_bias, lengths, seq_len)
     all_queries = lax.all_gather(queries, "enc", axis=0, tiled=True)

time: 363 us -> 553 us (1.52)
  waiting for transfers between devices: 248 us -> 423 us
  starting transfers between devices: 0.19 us -> 8.9 us
  local copies, waits for them, and re-layouts: 0.03 us -> 6.68 us
    all_to_all x0 -> x1, waiting for transfers between devices: none -> 249 us  [gather_from_all(): lax.all_to_all(jnp.tile(shard, repeats), axis, split_axis=dim, concat_axi...]
    all_gather x1 -> x0, waiting for transfers between devices: 82.1 us -> none  [per_device(): lax.all_gather(head_weight, 'enc', axis=0, tiled=True)]
    all_gather x1, waiting for transfers between devices: 41.4 us -> 58.3 us  [project(): lax.all_gather(dense_weight, 'enc', axis=0, tiled=True)]
    all_gather x1, waiting for transfers between devices: 9.17 us -> 0.02 us  [per_device(): all_queries = lax.all_gather(queries, 'enc', axis=0, tiled=True)]
    all_to_all x0 -> x1, starting transfers between devices: none -> 8.75 us  [gather_from_all(): lax.all_to_all(jnp.tile(shard, repeats), axis, split_axis=dim, concat_axi...]
    another operation x0 -> x1, local copies, waits for them, and re-layouts: none -> 6.65 us  [gather_from_all(): jnp.tile(shard, repeats)]
  transfers between devices with their start and end apart: 5 -> 5, of which waited for: 5 -> 4; matrix products, arithmetic and copies ran while one was open for 12% -> 8% of each run, Pallas kernels for 0% -> 0%
where the time goes in v1:
time: 553 us
  waiting for transfers between devices  423 us (76%)
  blocking collectives  50.5 us (9%)
  matrix products  37.7 us (7%)
  between operations  15.6 us (3%)
  other arithmetic  10.6 us (2%)
  starting transfers between devices  8.9 us (2%)
  local copies, waits for them, and re-layouts  6.68 us (1%)
    all_to_all x1, waiting for transfers between devices, gather_from_all(): lax.all_to_all(jnp.tile(shard, repeats), axis, split_axis=dim, concat_axi...  249 us
    reduce_scatter x1, waiting for transfers between devices, per_device(): lax.psum_scatter(jnp.dot(own_grad, pass_reps, preferred_element_type=jnp....  61.8 us
    all_gather x1, waiting for transfers between devices, project(): lax.all_gather(dense_weight, 'enc', axis=0, tiled=True)  58.3 us
    all_gather x1, waiting for transfers between devices, per_device(): features_all = lax.all_gather(hidden, ('vocab', 'grp'), axis=1, tiled=True)  51.1 us
    psum x1, blocking collectives, per_device(): local_scores = lax.psum(partial_value, ('vocab', 'grp'))  34.6 us
    dot_general x1, matrix products, per_device(): jnp.dot(normed, gather_from_all(head_weight, 'enc', 0), preferred_element...  21.3 us
    all_gather x1, blocking collectives, per_device(): scores = lax.all_gather(local_scores, 'enc', axis=1, tiled=True)  15.9 us
  transfers between devices with their start and end apart: 5, of which 4 were waited for; matrix products, arithmetic and copies ran while one was open for 8% of the time, Pallas kernels for 0%

profile of v1, /device:TPU:2, one launch (start us, length us, event | category | flops | bytes accessed | tf_op | source)
XLA Modules:
  0.0 552.7 jit_solution(10954221380074742720)
XLA Ops:
  7.2 6.6 %tile.2 = bf16[16,64,7936]{2,1,0:T(8,128)(2,1)} broadcast(bf16[64,7936]{1,0:T(8,128)(2,1)} %param.9), dimensions={1,2} | broadcast | bytes 17268736 | tf_op jit(solution)/shard_map/tile | solution.py:11
  13.8 0.0 copy-start.3
  13.8 8.7 %all-to-all-start = ((bf16[16,64,7936]{2,1,0:T(8,128)(2,1)}), bf16[16,64,7936]{2,1,0:T(8,128)(2,1)}, u32[]{:S(2)}, u32[]{:S(2)}) async-start(bf16[16,64,7936]{2,1,0:T(8,128)(2,1)} %tile.2), calls=%async_computation | async-start | bytes 32505856 | tf_op jit(solution)/shard_map/all_to_all | solution.py:10
  22.6 0.0 all-gather.5.cloned.1.call-start
  22.6 0.7 all-gather.5.cloned.1.call-update
  23.3 0.0 all-gather.7.cloned.1.call-start
  23.4 0.7 all-gather.7.cloned.1.call-update
  24.1 0.0 all-gather.9.cloned.1.call-start
  24.1 0.7 all-gather.9.cloned.1.call-update
  24.8 0.0 reduce-scatter.2.cloned.1.call-start
  24.8 0.0 copy-done.3
  24.9 0.1 iota_compare_fusion.1
  24.9 0.0 copy-done.1
  24.9 51.1 %all-gather.5.cloned.1.call-done = bf16[768,1024]{0,1:T(8,128)(2,1)} async-done(((bf16[768,64]{0,1:T(8,128)(2,1)}), bf16[768,1024]{0,1:T(8,128)(2,1)}) %all-gather.5.cloned.1.call-update) | async-done | bytes 1572880 | tf_op jit(solution)/shard_map/all_gather | solution.py:58
  76.1 58.3 %all-gather.7.cloned.1.call-done = bf16[1024,1024]{1,0:T(8,128)(2,1)} async-done(((bf16[64,1024]{1,0:T(8,128)(2,1)}), bf16[1024,1024]{1,0:T(8,128)(2,1)}) %all-gather.7.cloned.1.call-update) | async-done | bytes 2097168 | tf_op jit(solution)/shard_map/all_gather | solution.py:25
  134.4 10.5 %fusion.17 = (f32[768]{0:T(1024)S(1)}, f32[768,1024]{1,0:T(8,128)S(1)}) fusion(bf16[768,1024]{0,1:T(8,128)(2,1)} %all-gather.5.cloned.1.call-done, bf16[1024,1024]{1,0:T(8,128)(2,1)} %all-gather.7.cloned.1.call-done), kind=kOutput, calls=%fused_computation.41 | convolution fusion | flops 1661730048 | bytes 6818816 | tf_op jit(solution)/shard_map/dot_general | solution.py:23
  145.0 0.0 copy-start.2
  145.0 0.4 multiply_reduce_fusion
  145.4 249.2 %all-to-all-done = bf16[16,64,7936]{2,1,0:T(8,128)(2,1)} async-done(((bf16[16,64,7936]{2,1,0:T(8,128)(2,1)}), bf16[16,64,7936]{2,1,0:T(8,128)(2,1)}, u32[]{:S(2)}, u32[]{:S(2)}) %all-to-all-start) | async-done | bytes 16252960 | tf_op jit(solution)/shard_map/all_to_all | solution.py:10
  394.7 0.0 copy-done.2
  394.7 21.3 %convolution_add_fusion = f32[768,7936]{1,0:T(8,128)} fusion(bf16[1024,7936]{1,0:T(8,128)(2,1)} %bitcast, f32[7936]{0:T(1024)S(1)} %copy-done.2, f32[768,1024]{1,0:T(8,128)S(1)} %get-tuple-element.8, f32[768]{0:T(1024)S(1)} %add_rsqrt_fusion, f32[768]{0:T(1024)S(1)} %broadcast_multiply_fusion), kind=kOutput, calls=%fused_computation.1 | convolution fusion | flops 12490702848 | bytes 43815936 | tf_op jit(solution)/shard_map/dot_general | solution.py:60
  416.0 9.4 %select_reduce_fusion = f32[3,7936]{1,0:T(4,128)S(1)} fusion(f32[3,256,7936]{2,1,0:T(8,128)} %bitcast.15, pred[3,256]{1,0:T(4,128)(4,1)S(1)} %iota_compare_fusion.1), kind=kLoop, calls=%fused_computation | loop fusion | flops 12165888 | bytes 24475392 | tf_op jit(solution)/shard_map/reduce_max | solution.py:37
  425.4 0.0 all-gather.9.cloned.1.call-done
  425.4 2.2 convolution_bitcast_fusion
  427.6 34.6 %psum.7 = f32[128,3]{0,1:T(4,128)S(1)} all-reduce(f32[128,3]{0,1:T(4,128)S(1)} %convolution_bitcast_fusion), channel_id=1, replica_groups=mesh['enc'=16,'vocab'=8,'grp'=2] {'vocab','grp'}, use_global_device_ids=true, to_apply=%region_3.4 | all-reduce | flops 384 | bytes 3072 | tf_op jit(solution)/shard_map/psum | solution.py:68
  462.2 15.9 %all-gather = f32[16,3,128]{2,1,0:T(4,128)S(1)} all-gather(f32[1,3,128]{2,1,0:T(4,128)S(1)} %bitcast.18), channel_id=1, replica_groups=mesh['enc'=16,'vocab'=8,'grp'=2] {'enc'}, dimensions={0}, use_global_device_ids=true | all-gather | bytes 26112 | tf_op jit(solution)/shard_map/all_gather | solution.py:69
  478.2 0.6 subtract_reduce_fusion
  478.8 2.7 fusion.14
  481.5 0.0 reduce-scatter.2.cloned.1.call-update
  482.1 0.0 copy-done
  482.2 1.0 fusion.20
  483.2 61.8 %reduce-scatter.2.cloned.1.call-done = f32[8,7936]{1,0:T(8,128)} async-done(((f32[128,7936]{1,0:T(8,128)}), f32[8,7936]{1,0:T(8,128)}) %reduce-scatter.2.cloned.1.call-update) | async-done | bytes 253968 | tf_op jit(solution)/shard_map/reduce_scatter | solution.py:73
  (8 shorter events, 0.1 us)
Async XLA Ops:
  13.8 11.0 %copy-start.3 = (s32[3]{0:T(128)S(1)}, s32[3]{0:T(128)}, u32[]{:S(2)}) copy-start(s32[3]{0:T(128)} %param.11) | copy-start | bytes 40
  13.8 11.1 %copy-start.1 = (s32[128]{0:T(128)S(1)}, s32[128]{0:T(128)}, u32[]{:S(2)}) copy-start(s32[128]{0:T(128)} %param.13) | copy-start | bytes 1540
  13.8 380.9 %all-to-all-start = ((bf16[16,64,7936]{2,1,0:T(8,128)(2,1)}), bf16[16,64,7936]{2,1,0:T(8,128)(2,1)}, u32[]{:S(2)}, u32[]{:S(2)}) async-start(bf16[16,64,7936]{2,1,0:T(8,128)(2,1)} %tile.2), calls=%async_computation | async-start | bytes 32505856 | tf_op jit(solution)/shard_map/all_to_all | solution.py:10
  22.6 53.5 %all-gather.5.cloned.1.call-start = ((), (), s32[]{:S(2)}) async-start(), calls=%async_computation.2 | async-start | bytes 1671168 | tf_op jit(solution)/shard_map/all_gather | solution.py:58
  23.3 111.1 %all-gather.7.cloned.1.call-start = ((), (), s32[]{:S(2)}) async-start(), calls=%async_computation.3 | async-start | bytes 2228224 | tf_op jit(solution)/shard_map/all_gather | solution.py:25
  24.1 401.4 %all-gather.9.cloned.1.call-start = ((), (), s32[]{:S(2)}) async-start(), calls=%async_computation.4 | async-start | bytes 2158592 | tf_op jit(solution)/shard_map/all_gather | solution.py:64
  24.8 520.2 %reduce-scatter.2.cloned.1.call-start = ((), (), s32[]{:S(2)}) async-start(), calls=%async_computation.5 | async-start | bytes 4317184 | tf_op jit(solution)/shard_map/reduce_scatter | solution.py:73
  145.0 249.7 %copy-start.2 = (f32[7936]{0:T(1024)S(1)}, f32[7936]{0:T(1024)}, u32[]{:S(2)}) copy-start(f32[7936]{0:T(1024)} %param.10) | copy-start | bytes 95236
  478.8 3.3 copy-start
Sparse Core Ops, SparseCore 0:
  25.9 50.1 all-gather.4
  77.9 56.4 all-gather.6
  136.3 79.5 all-gather.8
  481.6 63.3 reduce-scatter.1
